TPU v7x, 32 devices: a whole 2x2x4 slice. The times are simulated.
32 devices in a mesh: rows: 8 (over y, x, core), cols: 4 (over z).
Axes of the slice: x: 2, y: 2, z: 4, core: 2. Of those that a mesh axis runs over, the one named last changes fastest.
Arguments:
- white_real: float32 [4096, 4096], P('rows', 'cols'), may hold values from -6 to 6
- white_imag: float32 [4096, 4096], P('rows', 'cols'), may hold values from -6 to 6
- covariates: bfloat16 [16, 4096, 4096], P(None, 'rows', 'cols'), may hold values from -6 to 6
- coefficients: float32 [16], replicated, may hold values from -0.9 to 0.9
- counts: int32 [4096, 4096], P('rows', 'cols'), may hold values from 0 to 5
- land_mask: int32 [4096, 4096], P('rows', 'cols'), may hold values from 0 to 1
- field_hyper: float32 [2], replicated, may hold values from 1 to 2
Outputs:
- step_real: float32 [4096, 4096], P('rows', 'cols')
- step_imag: float32 [4096, 4096], P('rows', 'cols')
- coef_grad: float32 [16], replicated
- objective: float32 [], replicated
All inputs are finite; a program needn't handle non-finite values.
Results may differ from a plain program's by a relative error of at most 0.0003.
Values sent between devices are 32-bit elements; how exact they have to be, the bound alone decides.
No kernel may reach another device: no remote copies, remote signals or barrier semaphores. Data moves between devices by JAX's collectives and lax.ppermute only.
A program may use at most 128 MiB of HBM per device.

v0:
```python
import math
import jax
import jax.numpy as jnp
from jax import lax
from jax.sharding import PartitionSpec as P

NG = 4096
lasso_weight = 0.02
ridge_weight = 0.1


def field_spectrum(field_hyper, wave_row, wave_col):
    amplitude = 0.2 * field_hyper[0]
    freq_range = field_hyper[1]
    radius = (wave_row[:, None] * wave_row[:, None] + wave_col[None, :] * wave_col[None, :]) / (
        freq_range * freq_range
    )
    return amplitude * (1.0 + NG / freq_range * jnp.power(1.0 + radius, -0.75))


def angle_table(left_len, right_len, modulus):
    product = lax.iota(jnp.int32, left_len)[:, None] * lax.iota(jnp.int32, right_len)[None, :]
    angles = (product % modulus).astype(jnp.float32) * (2.0 * math.pi / modulus)
    return (jnp.cos(angles), jnp.sin(angles))


def inverse_transform(pieces, want_real):
    highest = lax.Precision.HIGHEST
    components = pieces.shape[0]
    row_count = pieces.shape[1]
    length = pieces.shape[2]
    factor = 8
    others = length // factor
    shaped = pieces.reshape(components, row_count, others, factor)
    big_cos, big_sin = angle_table(others, others, others)

    def apply_big(table, block):
        return jnp.einsum("rnm,nk->rmk", block, table, precision=highest)

    if components == 2:
        real_mid = apply_big(big_cos, shaped[0]) - apply_big(big_sin, shaped[1])
        imag_mid = apply_big(big_sin, shaped[0]) + apply_big(big_cos, shaped[1])
    else:
        real_mid = apply_big(big_cos, shaped[0])
        imag_mid = apply_big(big_sin, shaped[0])
    tw_cos, tw_sin = angle_table(factor, others, length)
    real_tw = real_mid * tw_cos - imag_mid * tw_sin
    imag_tw = real_mid * tw_sin + imag_mid * tw_cos
    small_cos, small_sin = angle_table(factor, factor, factor)

    def apply_small(table, block):
        return jnp.einsum("rmk,mj->rjk", block, table, precision=highest)

    real_out = (apply_small(small_cos, real_tw) - apply_small(small_sin, imag_tw)).reshape(
        1, row_count, length
    )
    if want_real:
        return real_out
    imag_out = (apply_small(small_sin, real_tw) + apply_small(small_cos, imag_tw)).reshape(
        1, row_count, length
    )
    return jnp.concatenate([real_out, imag_out], axis=0)


def middle_step(spread):
    returned = lax.all_to_all(spread, "cols", split_axis=2, concat_axis=1, tiled=True)
    flipped = jnp.swapaxes(returned, 1, 2)
    return lax.all_to_all(flipped, "rows", split_axis=1, concat_axis=2, tiled=True)


def grid_transform(pieces, want_real):
    full_rows = lax.all_to_all(pieces, "cols", split_axis=1, concat_axis=2, tiled=True)
    halfway = inverse_transform(full_rows, False)
    columns = middle_step(halfway)
    second = inverse_transform(columns, want_real)
    blocks_out = lax.all_to_all(second, "rows", split_axis=2, concat_axis=1, tiled=True)
    return jnp.swapaxes(blocks_out, 1, 2) * (1.0 / NG)


def shards(white_real, white_imag, covariates, coefficients, counts, land_mask, field_hyper):
    highest = lax.Precision.HIGHEST
    rows_here = white_real.shape[0]
    cols_here = white_real.shape[1]
    freq_row = lax.axis_index("rows") * rows_here + lax.iota(jnp.int32, rows_here)
    freq_col = lax.axis_index("cols") * cols_here + lax.iota(jnp.int32, cols_here)
    wave_row = jnp.minimum(freq_row, NG - freq_row).astype(jnp.float32)
    wave_col = jnp.minimum(freq_col, NG - freq_col).astype(jnp.float32)
    spectrum = field_spectrum(field_hyper, wave_row, wave_col)
    scaled = jnp.stack([spectrum * white_real, spectrum * white_imag])
    latent = grid_transform(scaled, True)[0]
    cov_full = covariates.astype(jnp.float32)
    linear = jnp.einsum("j,jrc->rc", coefficients, cov_full, precision=highest)
    log_rate = linear + latent
    intensity = jnp.exp(log_rate)
    land_vals = land_mask.astype(jnp.float32)
    count_vals = counts.astype(jnp.float32)
    residual = land_vals * (intensity - count_vals)
    partial_coef = jnp.einsum("jrc,rc->j", cov_full, residual, precision=highest)
    partial_loss = jnp.sum(land_vals * (intensity - count_vals * log_rate)) + 0.5 * jnp.sum(
        white_real * white_real + white_imag * white_imag
    )
    adjoint = grid_transform(residual[None], False)
    total_coef, total_loss = lax.psum((partial_coef, partial_loss), ("rows", "cols"))
    per_cell = 1.0 / (NG * NG)
    coef_grad = (
        total_coef * per_cell + lasso_weight * jnp.sign(coefficients) + ridge_weight * coefficients
    )
    objective = (
        total_loss * per_cell
        + lasso_weight * jnp.sum(jnp.abs(coefficients))
        + 0.5 * ridge_weight * jnp.sum(coefficients * coefficients)
    )
    curvature = 1.0 + spectrum * spectrum
    step_real = (spectrum * adjoint[0] + white_real) / curvature
    step_imag = (white_imag - spectrum * adjoint[1]) / curvature
    return (step_real, step_imag, coef_grad, objective)


def solution(mesh):
    return jax.shard_map(
        shards,
        mesh=mesh,
        in_specs=(
            P("rows", "cols"),
            P("rows", "cols"),
            P(None, "rows", "cols"),
            P(),
            P("rows", "cols"),
            P("rows", "cols"),
            P(),
        ),
        out_specs=(P("rows", "cols"), P("rows", "cols"), P(), P()),
        check_vma=False,
    )
```

profile of v0, /device:TPU:0, one launch (start us, length us, event | category | flops | bytes accessed | tf_op | source)
XLA Modules:
  0.0 896.9 jit_solution(2084490301962304620)
XLA Ops:
  24.5 93.3 %all-to-all-done = f32[2,512,1024]{2,0,1:T(2,128)} async-done(((f32[2,512,1024]{2,0,1:T(2,128)}), f32[2,512,1024]{2,0,1:T(2,128)}, u32[]{:S(2)}, u32[]{:S(2)}) %all-to-all-start) | async-done | bytes 4194336 | tf_op jit(solution)/shard_map/all_to_all | solution.py:72
  127.4 10.3 %fusion.62 = f32[128,8,512]{2,0,1:T(8,128)} fusion(f32[128,512,8]{1,0,2:T(8,128)} %copy.151), kind=kOutput, calls=%fused_computation.88 | convolution fusion | flops 3224895488 | bytes 4194304 | tf_op jit(solution)/shard_map/rnm,nk->rmk/dot_general | solution.py:38
  137.6 8.4 fusion.74
  149.8 9.9 %convolution_subtract_fusion.2 = f32[128,8,512]{2,0,1:T(8,128)S(1)} fusion(f32[128,8,512]{2,0,1:T(8,128)} %fusion.74, f32[128,512,8]{1,0,2:T(8,128)S(1)} %copy.153), kind=kOutput, calls=%fused_computation.73 | convolution fusion | flops 3225419776 | bytes 6291456 | tf_op jit(solution)/shard_map/rnm,nk->rmk/dot_general | solution.py:38
  159.8 9.2 %multiply_subtract_fusion.3 = (f32[128,8,512]{2,0,1:T(8,128)S(1)}, f32[128,8,512]{2,0,1:T(8,128)S(1)}) fusion(f32[128,8,512]{2,0,1:T(8,128)S(1)} %convolution_subtract_fusion.2, f32[8,512]{1,0:T(8,128)S(1)} %get-tuple-element.32, f32[8,512]{1,0:T(8,128)S(1)} %get-tuple-element.33, f32[128,8,512]{2,0,1:T(8,128)S(1)} %copy-done.8, f32[128,512,8]{1,0,2:T(8,128)S(1)} %copy.153), kind=kOutput, calls=%fused_computation.41 | convolution fusion | flops 3228565504 | bytes 10518528 | tf_op jit(solution)/shard_map/rnm,nk->rmk/dot_general | solution.py:38
  192.2 95.3 %all_to_all.114 = f32[2,128,4096]{1,0,2:T(2,128)S(1)} all-to-all(f32[2,128,4096]{1,0,2:T(2,128)S(1)} %pad_maximum_fusion.1), channel_id=1, replica_groups=mesh['rows'=8,'cols'=4] {'cols'}, dimensions={2} | all-to-all | bytes 8388608 | tf_op jit(solution)/shard_map/all_to_all | solution.py:66
  302.5 52.9 %all_to_all.115 = f32[2,1024,512]{2,0,1:T(2,128)S(1)} all-to-all(f32[2,1024,512]{2,0,1:T(2,128)} %copy.164), channel_id=1, replica_groups=mesh['rows'=8,'cols'=4] {'rows'}, dimensions={1} | all-to-all | bytes 8388608 | tf_op jit(solution)/shard_map/all_to_all | solution.py:68
  362.6 10.3 %fusion.59 = f32[128,8,512]{2,0,1:T(8,128)} fusion(f32[128,512,8]{1,0,2:T(8,128)} %copy.167), kind=kOutput, calls=%fused_computation.85 | convolution fusion | flops 3224895488 | bytes 4194304 | tf_op jit(solution)/shard_map/rnm,nk->rmk/dot_general | solution.py:38
  372.9 8.4 fusion.71
  385.0 9.9 %convolution_subtract_fusion.1 = f32[128,8,512]{2,0,1:T(8,128)S(1)} fusion(f32[128,8,512]{2,0,1:T(8,128)} %fusion.71, f32[128,512,8]{1,0,2:T(8,128)S(1)} %copy.169), kind=kOutput, calls=%fused_computation.71 | convolution fusion | flops 3225419776 | bytes 6291456 | tf_op jit(solution)/shard_map/rnm,nk->rmk/dot_general | solution.py:38
  395.0 9.2 %multiply_subtract_fusion.2 = (f32[128,8,512]{2,0,1:T(8,128)S(1)}, f32[128,8,512]{2,0,1:T(8,128)S(1)}) fusion(f32[128,8,512]{2,0,1:T(8,128)S(1)} %convolution_subtract_fusion.1, f32[8,512]{1,0:T(8,128)S(1)} %get-tuple-element.32, f32[8,512]{1,0:T(8,128)S(1)} %get-tuple-element.33, f32[128,8,512]{2,0,1:T(8,128)S(1)} %copy-done.9, f32[128,512,8]{1,0,2:T(8,128)S(1)} %copy.169), kind=kOutput, calls=%fused_computation.37 | convolution fusion | flops 3228565504 | bytes 10518528 | tf_op jit(solution)/shard_map/rnm,nk->rmk/dot_general | solution.py:38
  415.8 22.7 %fusion = f32[1,512,1024]{2,0,1:T(1,128)} fusion(bf16[16,512,1024]{2,1,0:T(8,128)(2,1)} %param.9, f32[16]{0:T(128)S(1)} %copy-done.18), kind=kOutput, calls=%fused_computation.1 | convolution fusion | flops 100663296 | bytes 18874432 | tf_op jit(solution)/shard_map/j,jrc->rc/dot_general | solution.py:92
  449.1 48.1 %all_to_all.116 = f32[1,512,1024]{2,0,1:T(1,128)S(1)} all-to-all(f32[1,512,1024]{2,0,1:T(1,128)S(1)} %broadcast_in_dim.2), channel_id=1, replica_groups=mesh['rows'=8,'cols'=4] {'cols'}, dimensions={1} | all-to-all | bytes 4194304 | tf_op jit(solution)/shard_map/all_to_all | solution.py:72
  501.4 8.4 fusion.68
  509.8 9.0 %multiply_subtract_fusion.1 = (f32[128,8,512]{2,0,1:T(8,128)S(1)}, f32[128,8,512]{2,0,1:T(8,128)S(1)}) fusion(f32[128,8,512]{2,0,1:T(8,128)S(1)} %fusion.68, f32[8,512]{1,0:T(8,128)S(1)} %get-tuple-element.32, f32[8,512]{1,0:T(8,128)S(1)} %get-tuple-element.33, f32[128,512,8]{1,0,2:T(8,128)S(1)} %copy.177), kind=kOutput, calls=%fused_computation.33 | convolution fusion | flops 3228041216 | bytes 8421376 | tf_op jit(solution)/shard_map/rnm,nk->rmk/dot_general | solution.py:38
  542.0 94.5 %all_to_all.117 = f32[2,128,4096]{1,0,2:T(2,128)S(1)} all-to-all(f32[2,128,4096]{1,0,2:T(2,128)S(1)} %pad_maximum_fusion.2), channel_id=1, replica_groups=mesh['rows'=8,'cols'=4] {'cols'}, dimensions={2} | all-to-all | bytes 8388608 | tf_op jit(solution)/shard_map/all_to_all | solution.py:66
  651.5 54.8 %all_to_all.118 = f32[2,1024,512]{2,0,1:T(2,128)S(1)} all-to-all(f32[2,1024,512]{2,0,1:T(2,128)} %copy.187), channel_id=1, replica_groups=mesh['rows'=8,'cols'=4] {'rows'}, dimensions={1} | all-to-all | bytes 8388608 | tf_op jit(solution)/shard_map/all_to_all | solution.py:68
  713.5 10.3 %fusion.54 = f32[128,8,512]{2,0,1:T(8,128)} fusion(f32[128,512,8]{1,0,2:T(8,128)} %copy.190), kind=kOutput, calls=%fused_computation.80 | convolution fusion | flops 3224895488 | bytes 4194304 | tf_op jit(solution)/shard_map/rnm,nk->rmk/dot_general | solution.py:38
  723.8 8.4 fusion.66
  736.0 9.9 %convolution_subtract_fusion = f32[128,8,512]{2,0,1:T(8,128)S(1)} fusion(f32[128,8,512]{2,0,1:T(8,128)} %fusion.66, f32[128,512,8]{1,0,2:T(8,128)S(1)} %copy.192), kind=kOutput, calls=%fused_computation.69 | convolution fusion | flops 3225419776 | bytes 6291456 | tf_op jit(solution)/shard_map/rnm,nk->rmk/dot_general | solution.py:38
  745.9 9.2 %multiply_subtract_fusion = (f32[128,8,512]{2,0,1:T(8,128)S(1)}, f32[128,8,512]{2,0,1:T(8,128)S(1)}) fusion(f32[128,8,512]{2,0,1:T(8,128)S(1)} %convolution_subtract_fusion, f32[8,512]{1,0:T(8,128)S(1)} %get-tuple-element.32, f32[8,512]{1,0:T(8,128)S(1)} %get-tuple-element.33, f32[128,8,512]{2,0,1:T(8,128)S(1)} %copy-done.7, f32[128,512,8]{1,0,2:T(8,128)S(1)} %copy.192), kind=kOutput, calls=%fused_computation.29 | convolution fusion | flops 3228565504 | bytes 10518528 | tf_op jit(solution)/shard_map/rnm,nk->rmk/dot_general | solution.py:38
  784.5 7.5 multiply_reduce_fusion
  792.0 41.6 %all-to-all-done.7 = f32[2,128,4096]{1,0,2:T(2,128)} async-done(((f32[2,128,4096]{1,0,2:T(2,128)}), f32[2,128,4096]{1,0,2:T(2,128)}, u32[]{:S(2)}, u32[]{:S(2)}) %all-to-all-start.7) | async-done | bytes 4194336 | tf_op jit(solution)/shard_map/all_to_all | solution.py:76
  854.6 38.0 %all-reduce = (f32[16]{0:T(128)S(1)}, f32[]{:T(128)}) all-reduce(f32[16]{0:T(128)S(1)} %multiply_reduce_fusion, f32[]{:T(128)S(6)} %add.265), channel_id=1, replica_groups=mesh['rows'=8,'cols'=4] {'rows','cols'}, use_global_device_ids=true, to_apply=%region_0.1 | all-reduce | flops 17 | bytes 136 | tf_op jit(solution)/shard_map/psum | solution.py:103
  (109 shorter events, 209.3 us)
Async XLA Ops:
  3.9 4.5 copy-start.16
  4.0 4.5 copy-start.14
  17.9 99.9 %all-to-all-start = ((f32[2,512,1024]{2,0,1:T(2,128)}), f32[2,512,1024]{2,0,1:T(2,128)}, u32[]{:S(2)}, u32[]{:S(2)}) async-start(f32[2,512,1024]{2,0,1:T(2,128)} %pad_maximum_fusion), calls=%async_computation | async-start | bytes 8388608 | tf_op jit(solution)/shard_map/all_to_all | solution.py:72
  127.4 10.3 %copy-start.10 = (f32[128,512,8]{1,0,2:T(8,128)S(1)}, f32[128,512,8]{1,0,2:T(8,128)}, u32[]{:S(2)}) copy-start(f32[128,512,8]{1,0,2:T(8,128)} %copy.151) | copy-start | bytes 6291460
  137.6 8.4 copy-start.3
  149.8 10.0 %copy-start.8 = (f32[128,8,512]{2,0,1:T(8,128)S(1)}, f32[128,8,512]{2,0,1:T(8,128)}, u32[]{:S(2)}) copy-start(f32[128,8,512]{2,0,1:T(8,128)} %fusion.62) | copy-start | bytes 6291460
  362.6 10.3 %copy-start.11 = (f32[128,512,8]{1,0,2:T(8,128)S(1)}, f32[128,512,8]{1,0,2:T(8,128)}, u32[]{:S(2)}) copy-start(f32[128,512,8]{1,0,2:T(8,128)} %copy.167) | copy-start | bytes 6291460
  372.9 8.4 copy-start.4
  385.0 10.0 %copy-start.9 = (f32[128,8,512]{2,0,1:T(8,128)S(1)}, f32[128,8,512]{2,0,1:T(8,128)}, u32[]{:S(2)}) copy-start(f32[128,8,512]{2,0,1:T(8,128)} %fusion.59) | copy-start | bytes 6291460
  411.8 3.9 copy-start.18
  411.8 30.5 %all-to-all-start.3 = ((f32[1,128,4096]{1,0,2:T(1,128)}), f32[1,128,4096]{1,0,2:T(1,128)S(1)}, u32[]{:S(2)}, u32[]{:S(2)}) async-start(f32[1,128,4096]{1,0,2:T(1,128)} %bitcast.209), calls=%async_computation.3 | async-start | bytes 4194304 | tf_op jit(solution)/shard_map/all_to_all | solution.py:76
  442.3 2.1 copy-start.6
  442.3 2.2 copy-start.13
  447.6 1.4 copy-start
  713.5 10.3 %copy-start.12 = (f32[128,512,8]{1,0,2:T(8,128)S(1)}, f32[128,512,8]{1,0,2:T(8,128)}, u32[]{:S(2)}) copy-start(f32[128,512,8]{1,0,2:T(8,128)} %copy.190) | copy-start | bytes 6291460
  723.8 8.4 copy-start.5
  736.0 10.0 %copy-start.7 = (f32[128,8,512]{2,0,1:T(8,128)S(1)}, f32[128,8,512]{2,0,1:T(8,128)}, u32[]{:S(2)}) copy-start(f32[128,8,512]{2,0,1:T(8,128)} %fusion.54) | copy-start | bytes 6291460
  779.8 4.7 copy-start.1
  779.8 53.8 %all-to-all-start.7 = ((f32[2,128,4096]{1,0,2:T(2,128)}), f32[2,128,4096]{1,0,2:T(2,128)}, u32[]{:S(2)}, u32[]{:S(2)}) async-start(f32[2,128,4096]{1,0,2:T(2,128)} %pad_maximum_fusion.3), calls=%async_computation.7 | async-start | bytes 8388608 | tf_op jit(solution)/shard_map/all_to_all | solution.py:76
  842.0 5.0 copy-start.2
  842.0 5.0 copy-start.15
  842.0 5.0 copy-start.17
where the time goes:
time: 906 us; the launch traced here: 897 us
  blocking collectives  384 us (42%)
  matrix products  198 us (22%)
  waiting for transfers between devices  139 us (15%)
  local copies, waits for them, and re-layouts  102 us (11%)
  other arithmetic  51.1 us (6%)
  starting transfers between devices  15.1 us (2%)
    all_to_all x2, blocking collectives, middle_step(): lax.all_to_all(spread, 'cols', split_axis=2, concat_axis=1, tiled=True)  190 us
    dot_general x14, matrix products, apply_big(): return jnp.einsum('rnm,nk->rmk', block, table, precision=highest)  131 us
    all_to_all x2, blocking collectives, middle_step(): lax.all_to_all(flipped, 'rows', split_axis=1, concat_axis=2, tiled=True)  108 us
    all_to_all x1, waiting for transfers between devices, grid_transform(): lax.all_to_all(pieces, 'cols', split_axis=1, concat_axis=2, tiled=True)  93.3 us
    all_to_all x1, blocking collectives, grid_transform(): lax.all_to_all(pieces, 'cols', split_axis=1, concat_axis=2, tiled=True)  48.1 us
    all_to_all x2, waiting for transfers between devices, grid_transform(): lax.all_to_all(second, 'rows', split_axis=2, concat_axis=1, tiled=True)  45.5 us
    dot_general x14, matrix products, apply_small(): return jnp.einsum('rmk,mj->rjk', block, table, precision=highest)  44.6 us
    psum x1, blocking collectives, shards(): lax.psum((partial_coef, partial_loss), ('rows', 'cols'))  38 us
  transfers between devices with their start and end apart: 3, of which 3 were waited for; matrix products, arithmetic and copies ran while one was open for 3% of the time, Pallas kernels for 0%

commit v1 on v0

--- a/solution.py
+++ b/solution.py
@@ -3,10 +3,27 @@
 import jax.numpy as jnp
 from jax import lax
 from jax.sharding import PartitionSpec as P
+from jax.lax import axis_index, ppermute, psum
 
 NG = 4096
 lasso_weight = 0.02
 ridge_weight = 0.1
+
+
+def manage_the_signs(local_array, array_dim, q_in):
+    v_next = local_array.shape
+    low = local_array.reshape(
+        *v_next[:array_dim], q_in, v_next[array_dim] // q_in, *v_next[array_dim + 1 :]
+    )
+    return jnp.moveaxis(low, array_dim, 0)
+
+
+def wait_the_ports(work_x, dim_i):
+    work_x = jnp.moveaxis(work_x, 0, dim_i)
+    item_now = work_x.shape
+    return work_x.reshape(
+        *item_now[:dim_i], item_now[dim_i] * item_now[dim_i + 1], *item_now[dim_i + 2 :]
+    )
 
 
 def field_spectrum(field_hyper, wave_row, wave_col):
@@ -69,7 +86,18 @@
 
 
 def grid_transform(pieces, want_real):
-    full_rows = lax.all_to_all(pieces, "cols", split_axis=1, concat_axis=2, tiled=True)
+    newest, arr_now = (psum(1, "cols"), axis_index("cols"))
+    out_arr = manage_the_signs(pieces, 1, newest)
+    last = out_arr
+    for s in range(1, newest):
+        built, kept_arr = ((arr_now + s) % newest, (arr_now - s) % newest)
+        part_next = lax.dynamic_index_in_dim(out_arr, built, 0)
+        entries = []
+        for pp in range(newest):
+            entries.append((pp, (pp + s) % newest))
+        y2 = ppermute(part_next, axis_name="cols", perm=entries)
+        last = lax.dynamic_update_slice_in_dim(last, y2, kept_arr, axis=0)
+    full_rows = wait_the_ports(last, 2)
     halfway = inverse_transform(full_rows, False)
     columns = middle_step(halfway)
     second = inverse_transform(columns, want_real)

time: 906 us -> 907 us (level)
  waiting for transfers between devices: 139 us -> 94.2 us
  blocking collectives: 384 us -> 421 us
  matrix products: 198 us -> 215 us
    all_to_all x1 -> x0, waiting for transfers between devices: 93.3 us -> none  [grid_transform(): lax.all_to_all(pieces, 'cols', split_axis=1, concat_axis=2, tiled=True)]
    ppermute x0 -> x6, waiting for transfers between devices: none -> 90.3 us  [grid_transform(): y2 = ppermute(part_next, axis_name='cols', perm=entries)]
    all_to_all x2 -> x1, waiting for transfers between devices: 45.5 us -> 3.89 us  [grid_transform(): lax.all_to_all(second, 'rows', split_axis=2, concat_axis=1, tiled=True)]
    all_to_all x2, blocking collectives: 190 us -> 223 us  [middle_step(): lax.all_to_all(spread, 'cols', split_axis=2, concat_axis=1, tiled=True)]
    dot_general x14, matrix products: 44.6 us -> 57 us  [apply_small(): return jnp.einsum('rmk,mj->rjk', block, table, precision=highest)]
    another operation x2 -> x0, other arithmetic: 9.58 us -> none  [shards(): scaled = jnp.stack([spectrum * white_real, spectrum * white_imag])]
  transfers between devices with their start and end apart: 3 -> 7, of which waited for: 3 -> 6; matrix products, arithmetic and copies ran while one was open for 3% -> 4% of each run, Pallas kernels for 0% -> 0%
where the time goes in v1:
time: 907 us; the launch traced here: 903 us
  blocking collectives  421 us (46%)
  matrix products  215 us (24%)
  local copies, waits for them, and re-layouts  106 us (12%)
  waiting for transfers between devices  94.2 us (10%)
  other arithmetic  46.6 us (5%)
  starting transfers between devices  12 us (1%)
    all_to_all x2, blocking collectives, middle_step(): lax.all_to_all(spread, 'cols', split_axis=2, concat_axis=1, tiled=True)  223 us
    dot_general x14, matrix products, apply_big(): return jnp.einsum('rnm,nk->rmk', block, table, precision=highest)  135 us
    all_to_all x2, blocking collectives, middle_step(): lax.all_to_all(flipped, 'rows', split_axis=1, concat_axis=2, tiled=True)  108 us
    ppermute x6, waiting for transfers between devices, grid_transform(): y2 = ppermute(part_next, axis_name='cols', perm=entries)  90.3 us
    dot_general x14, matrix products, apply_small(): return jnp.einsum('rmk,mj->rjk', block, table, precision=highest)  57 us
    all_to_all x1, blocking collectives, grid_transform(): lax.all_to_all(second, 'rows', split_axis=2, concat_axis=1, tiled=True)  51.6 us
    psum x1, blocking collectives, shards(): lax.psum((partial_coef, partial_loss), ('rows', 'cols'))  37.9 us
    dot_general x1, matrix products, shards(): linear = jnp.einsum('j,jrc->rc', coefficients, cov_full, precision=highest)  22.7 us
  transfers between devices with their start and end apart: 7, of which 6 were waited for; matrix products, arithmetic and copies ran while one was open for 4% of the time, Pallas kernels for 0%

profile of v1, /device:TPU:0, one launch (start us, length us, event | category | flops | bytes accessed | tf_op | source)
XLA Modules:
  0.0 902.9 jit_solution(6545684004581918749)
XLA Ops:
  20.4 19.9 %collective-permute-done = f32[1,2,128,1024]{3,2,0,1:T(8,128)} collective-permute-done((f32[1,2,128,1024]{3,2,0,1:T(8,128)}, f32[1,2,128,1024]{3,2,0,1:T(8,128)}, u32[]{:S(2)}, u32[]{:S(2)}) %collective-permute-start) | collective-permute-done | bytes 1048608 | tf_op jit(solution)/shard_map/ppermute | solution.py:98
  41.6 42.8 %collective-permute-done.1 = f32[1,2,128,1024]{3,2,0,1:T(8,128)} collective-permute-done((f32[1,2,128,1024]{3,2,0,1:T(8,128)}, f32[1,2,128,1024]{3,2,0,1:T(8,128)}, u32[]{:S(2)}, u32[]{:S(2)}) %collective-permute-start.1) | collective-permute-done | bytes 1048608 | tf_op jit(solution)/shard_map/ppermute | solution.py:98
  91.9 10.3 %fusion.80 = f32[128,8,512]{2,0,1:T(8,128)} fusion(f32[128,512,8]{1,0,2:T(8,128)} %copy.147), kind=kOutput, calls=%fused_computation.112 | convolution fusion | flops 3224895488 | bytes 4194304 | tf_op jit(solution)/shard_map/rnm,nk->rmk/dot_general | solution.py:55
  102.2 8.4 fusion.68
  114.4 10.6 %convolution_subtract_fusion.2 = f32[128,8,512]{2,0,1:T(8,128)S(1)} fusion(f32[128,8,512]{2,0,1:T(8,128)} %fusion.80, f32[128,512,8]{1,0,2:T(8,128)S(1)} %copy.149), kind=kOutput, calls=%fused_computation.79 | convolution fusion | flops 3225419776 | bytes 6291456 | tf_op jit(solution)/shard_map/rnm,nk->rmk/dot_general | solution.py:55
  125.1 10.5 %multiply_subtract_fusion.3 = (f32[128,8,512]{2,0,1:T(8,128)S(1)}, f32[128,8,512]{2,0,1:T(8,128)S(1)}) fusion(f32[128,8,512]{2,0,1:T(8,128)S(1)} %convolution_subtract_fusion.2, f32[8,512]{1,0:T(8,128)S(1)} %get-tuple-element.38, f32[8,512]{1,0:T(8,128)S(1)} %get-tuple-element.39, f32[128,8,512]{2,0,1:T(8,128)S(1)} %copy-done.11, f32[128,512,8]{1,0,2:T(8,128)} %copy-done.1), kind=kOutput, calls=%fused_computation.48 | convolution fusion | flops 3228565504 | bytes 10518528 | tf_op jit(solution)/shard_map/rnm,nk->rmk/dot_general | solution.py:55
  164.0 117.3 %all_to_all.84 = f32[2,128,4096]{1,0,2:T(2,128)S(1)} all-to-all(f32[2,128,4096]{1,0,2:T(2,128)S(1)} %pad_maximum_fusion.1), channel_id=1, replica_groups=mesh['rows'=8,'cols'=4] {'cols'}, dimensions={2} | all-to-all | bytes 8388608 | tf_op jit(solution)/shard_map/all_to_all | solution.py:83
  296.3 53.3 %all_to_all.85 = f32[2,1024,512]{2,0,1:T(2,128)S(1)} all-to-all(f32[2,1024,512]{2,0,1:T(2,128)} %copy.160), channel_id=1, replica_groups=mesh['rows'=8,'cols'=4] {'rows'}, dimensions={1} | all-to-all | bytes 8388608 | tf_op jit(solution)/shard_map/all_to_all | solution.py:85
  356.8 10.3 %fusion.77 = f32[128,8,512]{2,0,1:T(8,128)} fusion(f32[128,512,8]{1,0,2:T(8,128)} %copy.163), kind=kOutput, calls=%fused_computation.109 | convolution fusion | flops 3224895488 | bytes 4194304 | tf_op jit(solution)/shard_map/rnm,nk->rmk/dot_general | solution.py:55
  367.1 8.4 fusion.65
  379.3 9.9 %convolution_subtract_fusion.1 = f32[128,8,512]{2,0,1:T(8,128)S(1)} fusion(f32[128,8,512]{2,0,1:T(8,128)} %fusion.77, f32[128,512,8]{1,0,2:T(8,128)S(1)} %copy.165), kind=kOutput, calls=%fused_computation.77 | convolution fusion | flops 3225419776 | bytes 6291456 | tf_op jit(solution)/shard_map/rnm,nk->rmk/dot_general | solution.py:55
  389.2 8.8 multiply_subtract_fusion.2
  409.8 22.7 %fusion = f32[1,512,1024]{2,0,1:T(1,128)} fusion(bf16[16,512,1024]{2,1,0:T(8,128)(2,1)} %param.9, f32[16]{0:T(128)S(1)} %copy-done.21), kind=kOutput, calls=%fused_computation.1 | convolution fusion | flops 100663296 | bytes 18874432 | tf_op jit(solution)/shard_map/j,jrc->rc/dot_general | solution.py:120
  461.7 20.0 %collective-permute-done.4 = f32[1,1,128,1024]{3,2,0,1:T(8,128)S(1)} collective-permute-done((f32[1,1,128,1024]{3,2,0,1:T(8,128)S(1)}, f32[1,1,128,1024]{3,2,0,1:T(8,128)S(1)}, u32[]{:S(2)}, u32[]{:S(2)}) %collective-permute-start.4) | collective-permute-done | bytes 524320 | tf_op jit(solution)/shard_map/ppermute | solution.py:98
  487.3 8.4 fusion.74
  495.7 10.5 %multiply_subtract_fusion.1 = (f32[128,8,512]{2,0,1:T(8,128)S(1)}, f32[128,8,512]{2,0,1:T(8,128)S(1)}) fusion(f32[128,8,512]{2,0,1:T(8,128)S(1)} %fusion.74, f32[8,512]{1,0:T(8,128)S(1)} %get-tuple-element.38, f32[8,512]{1,0:T(8,128)S(1)} %get-tuple-element.39, f32[128,512,8]{1,0,2:T(8,128)} %copy-done.13), kind=kOutput, calls=%fused_computation.40 | convolution fusion | flops 3228041216 | bytes 8421376 | tf_op jit(solution)/shard_map/rnm,nk->rmk/dot_general | solution.py:55
  534.3 105.7 %all_to_all.86 = f32[2,128,4096]{1,0,2:T(2,128)S(1)} all-to-all(f32[2,128,4096]{1,0,2:T(2,128)S(1)} %pad_maximum_fusion.2), channel_id=1, replica_groups=mesh['rows'=8,'cols'=4] {'cols'}, dimensions={2} | all-to-all | bytes 8388608 | tf_op jit(solution)/shard_map/all_to_all | solution.py:83
  655.0 55.1 %all_to_all.87 = f32[2,1024,512]{2,0,1:T(2,128)S(1)} all-to-all(f32[2,1024,512]{2,0,1:T(2,128)} %copy.183), channel_id=1, replica_groups=mesh['rows'=8,'cols'=4] {'rows'}, dimensions={1} | all-to-all | bytes 8388608 | tf_op jit(solution)/shard_map/all_to_all | solution.py:85
  717.3 10.3 %fusion.72 = f32[128,8,512]{2,0,1:T(8,128)} fusion(f32[128,512,8]{1,0,2:T(8,128)} %copy.186), kind=kOutput, calls=%fused_computation.104 | convolution fusion | flops 3224895488 | bytes 4194304 | tf_op jit(solution)/shard_map/rnm,nk->rmk/dot_general | solution.py:55
  727.6 8.4 fusion.60
  741.1 9.9 %convolution_subtract_fusion = f32[128,8,512]{2,0,1:T(8,128)S(1)} fusion(f32[128,8,512]{2,0,1:T(8,128)} %fusion.72, f32[128,512,8]{1,0,2:T(8,128)S(1)} %copy.188), kind=kOutput, calls=%fused_computation.75 | convolution fusion | flops 3225419776 | bytes 6291456 | tf_op jit(solution)/shard_map/rnm,nk->rmk/dot_general | solution.py:55
  751.0 10.7 %multiply_subtract_fusion = (f32[128,8,512]{2,0,1:T(8,128)S(1)}, f32[128,8,512]{2,0,1:T(8,128)S(1)}) fusion(f32[128,8,512]{2,0,1:T(8,128)S(1)} %convolution_subtract_fusion, f32[8,512]{1,0:T(8,128)S(1)} %get-tuple-element.38, f32[8,512]{1,0:T(8,128)S(1)} %get-tuple-element.39, f32[128,8,512]{2,0,1:T(8,128)S(1)} %copy-done.10, f32[128,512,8]{1,0,2:T(8,128)} %copy-done), kind=kOutput, calls=%fused_computation.36 | convolution fusion | flops 3228565504 | bytes 10518528 | tf_op jit(solution)/shard_map/rnm,nk->rmk/dot_general | solution.py:55
  790.1 51.6 %all_to_all.88 = f32[2,128,4096]{1,0,2:T(2,128)S(1)} all-to-all(f32[2,128,4096]{1,0,2:T(2,128)S(1)} %pad_maximum_fusion.3), channel_id=1, replica_groups=mesh['rows'=8,'cols'=4] {'rows'}, dimensions={2} | all-to-all | bytes 8388608 | tf_op jit(solution)/shard_map/all_to_all | solution.py:104
  860.5 37.9 %all-reduce = (f32[16]{0:T(128)S(1)}, f32[]{:T(128)}) all-reduce(f32[16]{0:T(128)S(1)} %multiply_reduce_fusion, f32[]{:T(128)S(6)} %add.346), channel_id=1, replica_groups=mesh['rows'=8,'cols'=4] {'rows','cols'}, use_global_device_ids=true, to_apply=%region_0.1 | all-reduce | flops 17 | bytes 136 | tf_op jit(solution)/shard_map/psum | solution.py:131
  (128 shorter events, 232.8 us)
Async XLA Ops:
  0.7 7.8 copy-start.17
  4.0 4.5 copy-start.19
  10.9 29.5 %collective-permute-start = (f32[1,2,128,1024]{3,2,0,1:T(8,128)}, f32[1,2,128,1024]{3,2,0,1:T(8,128)}, u32[]{:S(2)}, u32[]{:S(2)}) collective-permute-start(f32[1,2,128,1024]{3,2,0,1:T(8,128)} %get-tuple-element.28), channel_id=1, source_target_pairs={{0,1},{1,2},{2,3},{3,0},{4,5},{5,6},{6,7},{7,4},{8,9},{9,10},{10,1... | collective-permute-start | bytes 3145736 | tf_op jit(solution)/shard_map/ppermute | solution.py:98
  13.9 70.6 %collective-permute-start.1 = (f32[1,2,128,1024]{3,2,0,1:T(8,128)}, f32[1,2,128,1024]{3,2,0,1:T(8,128)}, u32[]{:S(2)}, u32[]{:S(2)}) collective-permute-start(f32[1,2,128,1024]{3,2,0,1:T(8,128)} %get-tuple-element.29), channel_id=1, source_target_pairs={{0,2},{1,3},{2,0},{3,1},{4,6},{5,7},{6,4},{7,5},{8,10},{9,11},{10,... | collective-permute-start | bytes 3145736 | tf_op jit(solution)/shard_map/ppermute | solution.py:98
  16.5 69.3 %collective-permute-start.2 = (f32[1,2,128,1024]{3,2,0,1:T(8,128)}, f32[1,2,128,1024]{3,2,0,1:T(8,128)S(1)}, u32[]{:S(2)}, u32[]{:S(2)}) collective-permute-start(f32[1,2,128,1024]{3,2,0,1:T(8,128)} %get-tuple-element.27), channel_id=1, source_target_pairs={{0,3},{1,0},{2,1},{3,2},{4,7},{5,4},{6,5},{7,6},{8,11},{9,8},{10,9... | collective-permute-start | bytes 3145736 | tf_op jit(solution)/shard_map/ppermute | solution.py:98
  91.9 10.3 %copy-start.14 = (f32[128,512,8]{1,0,2:T(8,128)S(1)}, f32[128,512,8]{1,0,2:T(8,128)}, u32[]{:S(2)}) copy-start(f32[128,512,8]{1,0,2:T(8,128)} %copy.147) | copy-start | bytes 6291460
  102.2 8.4 copy-start.4
  114.4 10.7 %copy-start.1 = (f32[128,512,8]{1,0,2:T(8,128)}, f32[128,512,8]{1,0,2:T(8,128)S(1)}, u32[]{:S(2)}) copy-start(f32[128,512,8]{1,0,2:T(8,128)S(1)} %copy.149) | copy-start | bytes 6291460
  114.4 10.7 %copy-start.11 = (f32[128,8,512]{2,0,1:T(8,128)S(1)}, f32[128,8,512]{2,0,1:T(8,128)}, u32[]{:S(2)}) copy-start(f32[128,8,512]{2,0,1:T(8,128)} %fusion.68) | copy-start | bytes 6291460
  155.9 3.1 copy-start.7
  356.8 10.3 %copy-start.15 = (f32[128,512,8]{1,0,2:T(8,128)S(1)}, f32[128,512,8]{1,0,2:T(8,128)}, u32[]{:S(2)}) copy-start(f32[128,512,8]{1,0,2:T(8,128)} %copy.163) | copy-start | bytes 6291460
  367.1 8.4 copy-start.5
  379.3 9.9 %copy-start.12 = (f32[128,8,512]{2,0,1:T(8,128)S(1)}, f32[128,8,512]{2,0,1:T(8,128)}, u32[]{:S(2)}) copy-start(f32[128,8,512]{2,0,1:T(8,128)} %fusion.65) | copy-start | bytes 6291460
  405.6 4.2 copy-start.21
  405.6 30.7 %all-to-all-start.2 = ((f32[1,128,4096]{1,0,2:T(1,128)}), f32[1,128,4096]{1,0,2:T(1,128)S(1)}, u32[]{:S(2)}, u32[]{:S(2)}) async-start(f32[1,128,4096]{1,0,2:T(1,128)} %bitcast.215), calls=%async_computation.2 | async-start | bytes 4194304 | tf_op jit(solution)/shard_map/all_to_all | solution.py:104
  446.5 14.9 %collective-permute-start.3 = (f32[1,1,128,1024]{3,2,0,1:T(8,128)S(1)}, f32[1,1,128,1024]{3,2,0,1:T(8,128)S(1)}, u32[]{:S(2)}, u32[]{:S(2)}) collective-permute-start(f32[1,1,128,1024]{3,2,0,1:T(8,128)S(1)} %constant_dynamic-slice_fusion.2), channel_id=1, source_target_pairs={{0,1},{1,2},{2,3},{3,0},{4,5},{5,6},{6,7},{7,4},{8,9},{9,10},{10,1... | collective-permute-start | bytes 1572872 | tf_op jit(solution)/shard_map/ppermute | solution.py:98
  461.6 20.2 %collective-permute-start.4 = (f32[1,1,128,1024]{3,2,0,1:T(8,128)S(1)}, f32[1,1,128,1024]{3,2,0,1:T(8,128)S(1)}, u32[]{:S(2)}, u32[]{:S(2)}) collective-permute-start(f32[1,1,128,1024]{3,2,0,1:T(8,128)S(1)} %get-tuple-element.31), channel_id=1, source_target_pairs={{0,2},{1,3},{2,0},{3,1},{4,6},{5,7},{6,4},{7,5},{8,10},{9,11},{10,... | collective-permute-start | bytes 1572872 | tf_op jit(solution)/shard_map/ppermute | solution.py:98
  461.7 20.5 %collective-permute-start.5 = (f32[1,1,128,1024]{3,2,0,1:T(8,128)S(1)}, f32[1,1,128,1024]{3,2,0,1:T(8,128)S(1)}, u32[]{:S(2)}, u32[]{:S(2)}) collective-permute-start(f32[1,1,128,1024]{3,2,0,1:T(8,128)S(1)} %get-tuple-element.30), channel_id=1, source_target_pairs={{0,3},{1,0},{2,1},{3,2},{4,7},{5,4},{6,5},{7,6},{8,11},{9,8},{10,9... | collective-permute-start | bytes 1572872 | tf_op jit(solution)/shard_map/ppermute | solution.py:98
  717.3 10.3 %copy-start.16 = (f32[128,512,8]{1,0,2:T(8,128)S(1)}, f32[128,512,8]{1,0,2:T(8,128)}, u32[]{:S(2)}) copy-start(f32[128,512,8]{1,0,2:T(8,128)} %copy.186) | copy-start | bytes 6291460
  727.6 8.4 copy-start.6
  741.1 9.9 %copy-start.10 = (f32[128,8,512]{2,0,1:T(8,128)S(1)}, f32[128,8,512]{2,0,1:T(8,128)}, u32[]{:S(2)}) copy-start(f32[128,8,512]{2,0,1:T(8,128)} %fusion.60) | copy-start | bytes 6291460
  847.9 5.0 copy-start.3
  847.9 5.0 copy-start.18
  847.9 5.0 copy-start.20
  (5 other events, 11.2 us)
